TPU v7x, 32 devices: a whole 2x2x4 slice. The times are simulated.
32 devices in a mesh: expert: 8 (over z, x), dp: 4 (over y, core).
Axes of the slice: x: 2, y: 2, z: 4, core: 2. Of those that a mesh axis runs over, the one named last changes fastest.
Arguments:
- features: bfloat16 [4096, 32, 64], P(('expert', 'dp')), may hold values from -1 to 1
- spacing: float32 [4096, 32], P(('expert', 'dp')), may hold values from 0.02 to 0.3
- targets: float32 [3, 4096], P(None, ('expert', 'dp')), may hold values from 0 to 1
- ray_length: int32 [4096], P(('expert', 'dp')), may hold values from 1 to 32, as said below
- cell_id: int32 [4096, 32], P(('expert', 'dp')), may hold values from 0 to 15, as said below
- slot_rank: int32 [4096, 32], P(('expert', 'dp')), may hold values from -1 to 383, as said below
- image_id: int32 [4096], P(('expert', 'dp')), may hold values from 0 to 511, as said below
- params: float32 [16, 848, 256], P('expert'), may hold values from -5 to 5
- first_moment: float32 [16, 848, 256], P('expert'), may hold values from -0.75 to 0.75
- second_moment: float32 [16, 848, 256], P('expert'), may hold values from 1e-06 to 0.01
- code_table: float32 [512, 64], P(('expert', 'dp')), may hold values from -6 to 6
- table_first: float32 [512, 64], P(('expert', 'dp')), may hold values from -0.75 to 0.75
- table_second: float32 [512, 64], P(('expert', 'dp')), may hold values from 1e-06 to 0.01
Outputs:
- ray_loss: float32 [4096], P(('expert', 'dp'))
- new_params: float32 [16, 848, 256], P('expert')
- new_first_moment: float32 [16, 848, 256], P('expert')
- new_second_moment: float32 [16, 848, 256], P('expert')
- new_code_table: float32 [512, 64], P(('expert', 'dp'))
- new_table_first: float32 [512, 64], P(('expert', 'dp'))
- new_table_second: float32 [512, 64], P(('expert', 'dp'))
Inputs may be any that keep to these rules, and one draw needn't show every extreme that they name: `ray_length`: rays form aligned blocks of 128, one a device, in the order of the axes expert then dp. In every block the lengths sum to 3072 and some ray has all 32 samples. `cell_id`: also given for samples at or beyond their ray's length, where it is unused. `slot_rank`: for a sample below its ray's length: its rank among the live samples of its block of 128 rays that have the same cell_id, counted ray by ray and along each ray; -1 for the other samples. No block has more than 384 live samples of one cell_id; in every block some cell_id has exactly 384, and one cell_id has 384 in every block. `image_id`: A ray of block b names an image from b * 16 to (b + 1) * 16 - 1.
All inputs are finite; a program needn't handle non-finite values.
Results may differ from a plain program's by a relative error of at most 0.0046.
Values may be sent and summed in bfloat16 or wider, within the bound.
A program may use at most 128 MiB of HBM per device.

v0:
```python
import jax
import jax.numpy as jnp
from jax import lax
from jax.sharding import PartitionSpec as P

NET_WIDTH = 256
CODE_WIDTH = 64
ENC_WIDTH = 64
LAYERS = 4
SAMPLES = 32
BETA_ONE = 0.9
BETA_TWO = 0.999
LEARN_RATE = 0.001
ADAM_EPS = 1e-08
CORRECT_ONE = 1.0 - 0.9**10
CORRECT_TWO = 1.0 - 0.999**10


def adam_update(param_now, gradient, moment_one, moment_two):
    new_one = BETA_ONE * moment_one + (1.0 - BETA_ONE) * gradient
    new_two = BETA_TWO * moment_two + (1.0 - BETA_TWO) * gradient * gradient
    update = LEARN_RATE * (new_one / CORRECT_ONE) / (jnp.sqrt(new_two / CORRECT_TWO) + ADAM_EPS)
    return (param_now - update, new_one, new_two)


def composite(raw_out, spacing, live_mask, targets):
    density = jax.nn.softplus(raw_out[0])
    colors = jax.nn.sigmoid(raw_out[1:4])
    optical = density * spacing * live_mask
    before = jnp.cumsum(optical, axis=1) - optical
    weight = jnp.exp(-before) * (1.0 - jnp.exp(-optical))
    render = jnp.sum(weight[None] * colors, axis=2)
    return 0.5 * jnp.sum((render - targets) ** 2, axis=0)


def place_rows(rows, slot_index, slots_all):
    blank = jnp.zeros((slots_all,) + rows.shape[1:], rows.dtype)
    return blank.at[slot_index].set(rows, mode="drop")


def pick_rows(buffer, slot_index):
    return jnp.take(buffer, slot_index, axis=0, mode="fill", fill_value=0)


def hidden_pass(weights_bf, inputs):
    head_row = ENC_WIDTH + (LAYERS - 1) * NET_WIDTH
    activations = [inputs]
    preacts = []
    current = inputs
    row_start = 0
    row_count = ENC_WIDTH
    for layer_index in range(LAYERS):
        matrix = weights_bf[:, row_start : row_start + row_count, :]
        bias_row = weights_bf[:, head_row + 9 + layer_index, :].astype(jnp.float32)
        preact = (
            jnp.einsum("enr,erw->enw", current, matrix, preferred_element_type=jnp.float32)
            + bias_row[:, None, :]
        )
        current = jnp.maximum(preact, 0.0).astype(jnp.bfloat16)
        preacts.append(preact)
        activations.append(current)
        row_start = row_start + row_count
        row_count = NET_WIDTH
    return (activations, preacts)


def hidden_grads(weights_bf, activations, preacts, upstream):
    weight_grads = [None] * LAYERS
    bias_grads = [None] * LAYERS
    for layer_index in reversed(range(LAYERS)):
        pre_grad = jnp.where(preacts[layer_index] > 0, upstream, 0.0).astype(jnp.bfloat16)
        weight_grads[layer_index] = jnp.einsum(
            "enr,enw->erw", activations[layer_index], pre_grad, preferred_element_type=jnp.float32
        )
        bias_grads[layer_index] = jnp.sum(pre_grad, axis=1, dtype=jnp.float32)
        if layer_index > 0:
            row_start = ENC_WIDTH + (layer_index - 1) * NET_WIDTH
            upstream = jnp.einsum(
                "enw,erw->enr",
                pre_grad,
                weights_bf[:, row_start : row_start + NET_WIDTH, :],
                preferred_element_type=jnp.float32,
            )
    return (weight_grads, bias_grads)


def assemble(weight_grads, bias_grads, hidden_grad, code_grad_head, bias_grad_head):
    held_count = hidden_grad.shape[0]
    pieces = list(weight_grads) + [
        hidden_grad,
        jnp.pad(code_grad_head, ((0, 0), (0, 0), (0, NET_WIDTH - CODE_WIDTH))),
        jnp.pad(bias_grad_head, ((0, 0), (0, NET_WIDTH - 4)))[:, None, :],
        jnp.stack(bias_grads, axis=1),
        jnp.zeros((held_count, 7 - LAYERS, NET_WIDTH), jnp.float32),
    ]
    return jnp.concatenate(pieces, axis=1)


def shards(
    features,
    spacing,
    targets,
    ray_length,
    cell_id,
    slot_rank,
    image_id,
    params,
    first_moment,
    second_moment,
    code_table,
    table_first,
    table_second,
):
    ray_rows = features.shape[0]
    sample_count = ray_rows * SAMPLES
    groups = lax.axis_size("expert")
    held_count = params.shape[0]
    experts_all = held_count * groups
    capacity = 2 * (sample_count * 3 // 4 // experts_all)
    slots_all = experts_all * capacity
    head_row = ENC_WIDTH + (LAYERS - 1) * NET_WIDTH
    weights_bf = params.astype(jnp.bfloat16)
    table_rows = code_table.shape[0]
    block_index = lax.axis_index("expert") * lax.axis_size("dp") + lax.axis_index("dp")
    local_image = image_id - block_index * table_rows
    picker = (local_image[:, None] == jnp.arange(table_rows, dtype=jnp.int32)[None, :]).astype(
        jnp.bfloat16
    )
    ray_code = jnp.dot(
        picker, code_table.astype(jnp.bfloat16), preferred_element_type=jnp.float32
    ).astype(jnp.bfloat16)
    position = jnp.arange(SAMPLES, dtype=jnp.int32)
    live_mask = (position[None, :] < ray_length[:, None]).astype(jnp.float32)
    flat_rank = slot_rank.reshape(sample_count)
    slot_index = jnp.where(
        flat_rank >= 0, cell_id.reshape(sample_count) * capacity + flat_rank, slots_all
    )
    positions = features.reshape(sample_count, ENC_WIDTH)
    sample_code = jnp.broadcast_to(ray_code[:, None, :], (ray_rows, SAMPLES, CODE_WIDTH)).reshape(
        sample_count, CODE_WIDTH
    )
    outgoing = place_rows(
        jnp.concatenate([positions, sample_code], axis=1), slot_index, slots_all
    ).reshape(experts_all, capacity, ENC_WIDTH + CODE_WIDTH)
    arrived = lax.all_to_all(outgoing, "expert", split_axis=0, concat_axis=1, tiled=True)
    hidden_head = weights_bf[:, head_row : head_row + 4, :]
    inputs = arrived[:, :, :ENC_WIDTH]
    code_rows = arrived[:, :, ENC_WIDTH:]
    activations, preacts = hidden_pass(weights_bf, inputs)
    raw_out = jnp.einsum(
        "enw,ecw->enc", activations[-1], hidden_head, preferred_element_type=jnp.float32
    )
    code_head = weights_bf[:, head_row + 4 : head_row + 8, :CODE_WIDTH]
    raw_out = raw_out + jnp.einsum(
        "enk,eck->enc", code_rows, code_head, preferred_element_type=jnp.float32
    )
    raw_out = raw_out + weights_bf[:, head_row + 8, :4].astype(jnp.float32)[:, None, :]
    returned = lax.all_to_all(raw_out, "expert", split_axis=1, concat_axis=0, tiled=True)
    raw_samples = pick_rows(returned.reshape(slots_all, 4), slot_index)
    raw_grid = raw_samples.T.reshape(4, ray_rows, SAMPLES)

    def loss_of(raw_in):
        return composite(raw_in, spacing, live_mask, targets)

    ray_loss, pullback = jax.vjp(loss_of, raw_grid)
    (raw_grad,) = pullback(jnp.ones_like(ray_loss))
    cotangent = raw_grad.reshape(4, sample_count).T.astype(jnp.bfloat16)
    cot_slots = place_rows(cotangent, slot_index, slots_all).reshape(experts_all, capacity, 4)
    cot_in = lax.all_to_all(cot_slots, "expert", split_axis=0, concat_axis=1, tiled=True)
    upstream = jnp.einsum("enc,ecw->enw", cot_in, hidden_head, preferred_element_type=jnp.float32)
    weight_grads, bias_grads = hidden_grads(weights_bf, activations, preacts, upstream)
    hidden_grad = jnp.einsum(
        "enc,enw->ecw", cot_in, activations[-1], preferred_element_type=jnp.float32
    )
    code_grad_head = jnp.einsum(
        "enc,enk->eck", cot_in, code_rows, preferred_element_type=jnp.float32
    )
    bias_grad_head = jnp.sum(cot_in, axis=1, dtype=jnp.float32)
    code_back = jnp.einsum("enc,eck->enk", cot_in, code_head, preferred_element_type=jnp.float32)
    code_back = code_back.reshape(held_count, groups * capacity // 2, 2 * CODE_WIDTH)
    code_slot_grad = lax.all_to_all(
        code_back, "expert", split_axis=1, concat_axis=0, tiled=True
    ).reshape(slots_all, CODE_WIDTH)
    local_grad = assemble(weight_grads, bias_grads, hidden_grad, code_grad_head, bias_grad_head)
    param_grad = lax.psum(local_grad, "dp")
    sample_code_grad = pick_rows(code_slot_grad, slot_index).reshape(ray_rows, SAMPLES, CODE_WIDTH)
    ray_code_grad = jnp.sum(sample_code_grad, axis=1)
    table_grad = lax.dot_general(
        picker.astype(jnp.float32),
        ray_code_grad,
        (((0,), (0,)), ((), ())),
        precision=lax.Precision.HIGHEST,
        preferred_element_type=jnp.float32,
    )
    new_params, new_first, new_second = adam_update(params, param_grad, first_moment, second_moment)
    new_table, new_table_first, new_table_second = adam_update(
        code_table, table_grad, table_first, table_second
    )
    return (
        ray_loss,
        new_params,
        new_first,
        new_second,
        new_table,
        new_table_first,
        new_table_second,
    )


def solution(mesh):
    return jax.shard_map(
        shards,
        mesh=mesh,
        in_specs=(
            P(("expert", "dp"), None, None),
            P(("expert", "dp"), None),
            P(None, ("expert", "dp")),
            P(("expert", "dp")),
            P(("expert", "dp"), None),
            P(("expert", "dp"), None),
            P(("expert", "dp")),
            P("expert", None, None),
            P("expert", None, None),
            P("expert", None, None),
            P(("expert", "dp"), None),
            P(("expert", "dp"), None),
            P(("expert", "dp"), None),
        ),
        out_specs=(
            P(("expert", "dp")),
            P("expert", None, None),
            P("expert", None, None),
            P("expert", None, None),
            P(("expert", "dp"), None),
            P(("expert", "dp"), None),
            P(("expert", "dp"), None),
        ),
        check_vma=False,
    )
```

profile of v0, /device:TPU:0, one launch (start us, length us, event | category | flops | bytes accessed | tf_op | source)
XLA Modules:
  0.0 286.6 jit_solution(14919669906394410517)
XLA Ops:
  13.4 13.5 %scatter_custom_fusion = bf16[6144,128]{1,0:T(8,128)(2,1)} fusion(s32[4096]{0:T(1024)S(1)} %bitcast.80, bf16[4096,64]{1,0:T(8,128)(2,1)} %bitcast.72, bf16[]{:T(256)} %constant.118, bf16[4096,64]{1,0:T(8,128)(2,1)S(1)} %bitcast.71, bf16[]{:T(256)} %constant.35.clone.1), kind=kCustom, calls=%fused_computation.37 | custom fusion | flops 2097152 | bytes 3145732 | tf_op jit(solution)/shard_map/scatter | solution.py:38
  26.9 7.6 %all-to-all-start = ((bf16[16,384,128]{2,1,0:T(8,128)(2,1)}), bf16[16,384,128]{2,1,0:T(8,128)(2,1)S(1)}, u32[]{:S(2)}, u32[]{:S(2)}) async-start(bf16[16,384,128]{2,1,0:T(8,128)(2,1)} %bitcast.68), calls=%async_computation | async-start | bytes 3145728 | tf_op jit(solution)/shard_map/all_to_all | solution.py:145
  35.6 35.9 %all-to-all-done = bf16[16,384,128]{2,1,0:T(8,128)(2,1)S(1)} async-done(((bf16[16,384,128]{2,1,0:T(8,128)(2,1)}), bf16[16,384,128]{2,1,0:T(8,128)(2,1)S(1)}, u32[]{:S(2)}, u32[]{:S(2)}) %all-to-all-start) | async-done | bytes 1572896 | tf_op jit(solution)/shard_map/all_to_all | solution.py:145
  73.4 4.1 %fusion.2 = (u8[3072,256]{1,0:T(8,128)(4,1)}, f32[2,3072,256]{2,1,0:T(8,128)S(1)}) fusion(f32[2,256]{1,0:T(2,128)S(1)} %bitcast.86, bf16[2,848,256]{2,1,0:T(8,128)(2,1)} %copy-done.9, bf16[2,3072,128]{1,2,0:T(8,128)(2,1)S(1)} %all_to_all.51), kind=kOutput, calls=%fused_computation.32 | convolution fusion | flops 209977344 | bytes 7931904 | tf_op jit(solution)/shard_map/enr,erw->enw/dot_general | solution.py:56
  77.5 3.1 %fusion.3 = (u8[3072,256]{1,0:T(8,128)(4,1)}, f32[2,3072,256]{2,1,0:T(8,128)S(1)}) fusion(f32[2,256]{1,0:T(2,128)S(1)} %get-tuple-element.38, bf16[2,848,256]{2,1,0:T(8,128)(2,1)S(1)} %copy-done.10, f32[2,3072,256]{2,1,0:T(8,128)S(1)} %get-tuple-element.28, f32[2,256]{1,0:T(2,128)S(1)} %bitcast.87), kind=kOutput, calls=%fused_computation.33 | convolution fusion | flops 818675712 | bytes 13635584 | tf_op jit(solution)/shard_map/enr,erw->enw/dot_general | solution.py:56
  80.6 3.1 %fusion.4 = (u8[3072,256]{1,0:T(8,128)(4,1)}, f32[2,3072,256]{2,1,0:T(8,128)S(1)}) fusion(f32[2,256]{1,0:T(2,128)S(1)} %get-tuple-element.37, bf16[2,848,256]{2,1,0:T(8,128)(2,1)S(1)} %copy-done.10, f32[2,3072,256]{2,1,0:T(8,128)S(1)} %get-tuple-element.26, f32[2,256]{1,0:T(2,128)S(1)} %get-tuple-element.38), kind=kOutput, calls=%fused_computation.34 | convolution fusion | flops 818675712 | bytes 13635584 | tf_op jit(solution)/shard_map/enr,erw->enw/dot_general | solution.py:56
  83.7 3.1 %fusion.5 = (u8[3072,256]{1,0:T(8,128)(4,1)}, f32[2,3072,256]{2,1,0:T(8,128)S(1)}) fusion(f32[2,256]{1,0:T(2,128)S(1)} %bitcast.83, bf16[2,848,256]{2,1,0:T(8,128)(2,1)S(1)} %copy-done.10, f32[2,3072,256]{2,1,0:T(8,128)S(1)} %get-tuple-element.24, f32[2,256]{1,0:T(2,128)S(1)} %get-tuple-element.37), kind=kOutput, calls=%fused_computation.35 | convolution fusion | flops 818675712 | bytes 13635584 | tf_op jit(solution)/shard_map/enr,erw->enw/dot_general | solution.py:56
  89.7 2.9 %copy.96 = f32[2,3072,4]{2,0,1:T(2,128)S(1)} copy(f32[2,3072,4]{1,2,0:T(4,128)S(1)} %fusion) | data formatting | bytes 196608 | tf_op jit(solution)/shard_map/add | solution.py:157
  92.6 5.6 %reshape.184 = f32[8,1,3072]{2,1,0:T(1,128)} reshape(f32[3072,2,4]{2,1,0:T(2,128)S(1)} %bitcast.65) | data formatting | bytes 196608
  98.2 4.2 %all-to-all-start.1 = ((f32[8,1,3072]{2,1,0:T(1,128)}), f32[8,1,3072]{2,1,0:T(1,128)S(1)}, u32[]{:S(2)}, u32[]{:S(2)}) async-start(f32[8,1,3072]{2,1,0:T(1,128)} %reshape.184), calls=%async_computation.1 | async-start | bytes 196608 | tf_op jit(solution)/shard_map/all_to_all | solution.py:158
  102.4 7.1 %all-to-all-done.1 = f32[8,1,3072]{2,1,0:T(1,128)S(1)} async-done(((f32[8,1,3072]{2,1,0:T(1,128)}), f32[8,1,3072]{2,1,0:T(1,128)S(1)}, u32[]{:S(2)}, u32[]{:S(2)}) %all-to-all-start.1) | async-done | bytes 98336 | tf_op jit(solution)/shard_map/all_to_all | solution.py:158
  110.9 6.6 %reshape.185 = f32[3072,2,4]{2,1,0:T(2,128)} reshape(f32[8,3072]{1,0:T(8,128)S(1)} %reduce.14) | data formatting | bytes 196608
  119.7 14.1 %gather_fusion = f32[4096,4]{1,0:T(8,128)} fusion(f32[6144,4]{1,0:T(8,128)S(1)} %bitcast.60, s32[4096]{0:T(1024)S(1)} %broadcast_clamp_fusion), kind=kCustom, calls=%fused_computation | custom fusion | bytes 147456 | tf_op jit(solution)/shard_map/jit(_take)/gather | solution.py:42
  138.3 11.4 %scatter_custom_fusion.1 = bf16[6144,4]{1,0:T(8,128)(2,1)S(1)} fusion(s32[4096]{0:T(1024)S(1)} %bitcast.82, bf16[4096,4]{1,0:T(8,128)(2,1)S(1)} %copy.113, bf16[]{:T(256)} %constant.35.clone.1), kind=kCustom, calls=%fused_computation.49 | custom fusion | bytes 49154 | tf_op jit(solution)/shard_map/scatter | solution.py:38
  150.4 9.3 %all_to_all.66 = bf16[16,384,4]{1,2,0:T(4,128)(2,1)S(1)} all-to-all(bf16[16,384,4]{1,2,0:T(4,128)(2,1)S(1)} %copy.114), channel_id=1, replica_groups=mesh['expert'=8,'dp'=4] {'expert'}, dimensions={0} | all-to-all | bytes 98304 | tf_op jit(solution)/shard_map/all_to_all | solution.py:169
  159.8 3.6 %fusion.16 = f32[2,4,256]{2,1,0:T(4,128)S(1)} fusion(bf16[2,3072,4]{1,2,0:T(4,128)(2,1)S(1)} %bitcast.73, f32[2,3072,256]{2,1,0:T(8,128)} %copy-done.3, f32[2,256]{1,0:T(2,128)S(1)} %bitcast.85), kind=kOutput, calls=%fused_computation.47 | convolution fusion | flops 17301504 | bytes 6350848 | tf_op jit(solution)/shard_map/enc,enw->ecw/dot_general | solution.py:172
  172.2 3.0 %convert_reduce_fusion.3 = (f32[2,256]{1,0:T(2,128)S(1)}, bf16[2,3072,256]{2,1,0:T(8,128)(2,1)}) fusion(bf16[2,3072,256]{2,1,0:T(8,128)(2,1)S(1)} %get-tuple-element.32, bf16[2,848,256]{2,1,0:T(8,128)(2,1)S(1)} %copy-done.11, u8[3072,256]{1,0:T(8,128)(4,1)S(1)} %copy-done.16), kind=kOutput, calls=%fused_computation.16 | convolution fusion | flops 817888768 | bytes 7342080 | tf_op jit(solution)/shard_map/enw,erw->enr/dot_general | solution.py:78
  176.7 7.0 %copy.121 = f32[2,1536,128]{2,0,1:T(2,128)} copy(f32[2,1536,128]{2,1,0:T(8,128)} %reshape.134) | data formatting | bytes 3145728 | tf_op jit(solution)/shard_map/reshape | solution.py:180
  183.7 3.6 %all-to-all-start.3 = ((f32[2,1536,128]{2,0,1:T(2,128)}), f32[2,1536,128]{2,0,1:T(2,128)S(1)}, u32[]{:S(2)}, u32[]{:S(2)}) async-start(f32[2,1536,128]{2,0,1:T(2,128)} %copy.121), calls=%async_computation.3 | async-start | bytes 3145728 | tf_op jit(solution)/shard_map/all_to_all | solution.py:181
  190.4 5.4 %fusion.12 = f32[2,256,256]{2,1,0:T(8,128)} fusion(bf16[2,3072,256]{2,1,0:T(8,128)(2,1)S(1)} %copy-done.13, f32[2,3072,256]{2,1,0:T(8,128)} %copy-done.1, f32[2,256]{1,0:T(2,128)S(1)} %get-tuple-element.38), kind=kOutput, calls=%fused_computation.43 | convolution fusion | flops 810024960 | bytes 9963520 | tf_op jit(solution)/shard_map/enr,enw->erw/dot_general | solution.py:72
  198.1 7.2 %concatenate.7 = f32[2,848,256]{2,1,0:T(8,128)} concatenate(f32[2,64,256]{2,1,0:T(8,128)S(1)} %fusion.24, f32[2,256,256]{2,1,0:T(8,128)} %fusion.10, f32[2,256,256]{2,1,0:T(8,128)} %fusion.12, f32[2,256,256]{2,1,0:T(8,128)} %fusion.14, f32[2,4,256]{2,1,0:T(4,128)S(1)} %fusion.16, f32[2,4,256]{2,1,0:T(4,128)S(1)} %pad.16, f32[2,1,256]{2,1,0:T(1,128)S(1)} %broadcast_in_dim.84, ...), dimensions={1} | concatenate | bytes 3473408 | tf_op jit(solution)/shard_map/concatenate | solution.py:96
  206.0 46.4 %all-reduce.6.cloned.1.call-done = f32[2,848,256]{2,1,0:T(8,128)} async-done(((f32[2,848,256]{2,1,0:T(8,128)}), f32[2,848,256]{2,1,0:T(8,128)}) %all-reduce.6.cloned.1.call-update) | async-done | bytes 1736720 | tf_op jit(solution)/shard_map/psum | solution.py:185
  252.4 5.5 %divide_subtract_fusion = (f32[2,848,256]{2,1,0:T(8,128)}, f32[2,848,256]{2,1,0:T(8,128)}, f32[2,848,256]{2,1,0:T(8,128)}) fusion(f32[2,848,256]{2,1,0:T(8,128)S(1)} %copy-done.5, f32[2,848,256]{2,1,0:T(8,128)} %all-reduce.6.cloned.1.call-done, f32[2,848,256]{2,1,0:T(8,128)} %param.21, f32[2,848,256]{2,1,0:T(8,128)} %param.22), kind=kLoop, calls=%fused_computation.30 | loop fusion | flops 5210112 | bytes 12156928 | tf_op jit(solution)/shard_map/sub | solution.py:23
  261.7 14.1 %gather_fusion.1 = f32[4096,64]{1,0:T(8,128)} fusion(f32[6144,64]{1,0:T(8,128)S(1)} %reshape.135, s32[4096]{0:T(1024)S(1)} %broadcast_clamp_fusion), kind=kCustom, calls=%fused_computation.1 | custom fusion | bytes 2113536 | tf_op jit(solution)/shard_map/jit(_take)/gather | solution.py:42
  (143 shorter events, 44.5 us)
Async XLA Ops:
  13.4 21.2 %copy-start.4 = (f32[2,848,256]{2,1,0:T(8,128)S(1)}, f32[2,848,256]{2,1,0:T(8,128)}, u32[]{:S(2)}) copy-start(f32[2,848,256]{2,1,0:T(8,128)} %param.20) | copy-start | bytes 5210116
  26.9 44.6 %all-to-all-start = ((bf16[16,384,128]{2,1,0:T(8,128)(2,1)}), bf16[16,384,128]{2,1,0:T(8,128)(2,1)S(1)}, u32[]{:S(2)}, u32[]{:S(2)}) async-start(bf16[16,384,128]{2,1,0:T(8,128)(2,1)} %bitcast.68), calls=%async_computation | async-start | bytes 3145728 | tf_op jit(solution)/shard_map/all_to_all | solution.py:145
  73.4 16.1 %copy-start.6 = (bf16[2,3072,128]{1,2,0:T(8,128)(2,1)}, bf16[2,3072,128]{1,2,0:T(8,128)(2,1)S(1)}, u32[]{:S(2)}) copy-start(bf16[2,3072,128]{1,2,0:T(8,128)(2,1)S(1)} %all_to_all.51) | copy-start | bytes 4718596
  73.4 4.1 %copy-start.10 = (bf16[2,848,256]{2,1,0:T(8,128)(2,1)S(1)}, bf16[2,848,256]{2,1,0:T(8,128)(2,1)}, u32[]{:S(2)}) copy-start(bf16[2,848,256]{2,1,0:T(8,128)(2,1)} %copy-done.9) | copy-start | bytes 2605060
  77.5 3.1 %copy-start = (f32[2,3072,256]{2,1,0:T(8,128)}, f32[2,3072,256]{2,1,0:T(8,128)S(1)}, u32[]{:S(2)}) copy-start(f32[2,3072,256]{2,1,0:T(8,128)S(1)} %get-tuple-element.28) | copy-start | bytes 18874372
  80.6 3.1 %copy-start.1 = (f32[2,3072,256]{2,1,0:T(8,128)}, f32[2,3072,256]{2,1,0:T(8,128)S(1)}, u32[]{:S(2)}) copy-start(f32[2,3072,256]{2,1,0:T(8,128)S(1)} %get-tuple-element.26) | copy-start | bytes 18874372
  83.7 3.1 %copy-start.2 = (f32[2,3072,256]{2,1,0:T(8,128)}, f32[2,3072,256]{2,1,0:T(8,128)S(1)}, u32[]{:S(2)}) copy-start(f32[2,3072,256]{2,1,0:T(8,128)S(1)} %get-tuple-element.24) | copy-start | bytes 18874372
  98.2 11.3 %all-to-all-start.1 = ((f32[8,1,3072]{2,1,0:T(1,128)}), f32[8,1,3072]{2,1,0:T(1,128)S(1)}, u32[]{:S(2)}, u32[]{:S(2)}) async-start(f32[8,1,3072]{2,1,0:T(1,128)} %reshape.184), calls=%async_computation.1 | async-start | bytes 196608 | tf_op jit(solution)/shard_map/all_to_all | solution.py:158
  119.7 16.6 %copy-start.20 = (f32[128,32]{0,1:T(8,128)S(1)}, f32[128,32]{0,1:T(8,128)}, u32[]{:S(2)}) copy-start(f32[128,32]{0,1:T(8,128)} %param.14) | copy-start | bytes 49156
  119.7 16.6 %copy-start.24 = (s32[128]{0:T(128)S(1)}, s32[128]{0:T(128)}, u32[]{:S(2)}) copy-start(s32[128]{0:T(128)} %param.16) | copy-start | bytes 1540
  133.8 2.9 %copy-start.25 = (f32[3,128]{1,0:T(4,128)S(1)}, f32[3,128]{1,0:T(4,128)}, u32[]{:S(2)}) copy-start(f32[3,128]{1,0:T(4,128)} %param.15) | copy-start | bytes 4612
  159.8 3.6 %copy-start.7 = (bf16[2,3072,128]{1,2,0:T(8,128)(2,1)S(1)}, bf16[2,3072,128]{1,2,0:T(8,128)(2,1)}, u32[]{:S(2)}) copy-start(bf16[2,3072,128]{1,2,0:T(8,128)(2,1)} %copy-done.6) | copy-start | bytes 4718596
  159.8 3.9 %copy-start.11 = (bf16[2,848,256]{2,1,0:T(8,128)(2,1)S(1)}, bf16[2,848,256]{2,1,0:T(8,128)(2,1)}, u32[]{:S(2)}) copy-start(bf16[2,848,256]{2,1,0:T(8,128)(2,1)} %copy-done.9) | copy-start | bytes 2605060
  172.1 3.1 %copy-start.14 = (bf16[2,3072,256]{2,1,0:T(8,128)(2,1)}, bf16[2,3072,256]{2,1,0:T(8,128)(2,1)S(1)}, u32[]{:S(2)}) copy-start(bf16[2,3072,256]{2,1,0:T(8,128)(2,1)S(1)} %get-tuple-element.32) | copy-start | bytes 9437188
  176.7 10.9 %copy-start.8 = (bf16[2,3072,128]{1,2,0:T(8,128)(2,1)S(1)}, bf16[2,3072,128]{1,2,0:T(8,128)(2,1)}, u32[]{:S(2)}) copy-start(bf16[2,3072,128]{1,2,0:T(8,128)(2,1)} %copy-done.6) | copy-start | bytes 4718596
  183.7 74.1 %all-to-all-start.3 = ((f32[2,1536,128]{2,0,1:T(2,128)}), f32[2,1536,128]{2,0,1:T(2,128)S(1)}, u32[]{:S(2)}, u32[]{:S(2)}) async-start(f32[2,1536,128]{2,0,1:T(2,128)} %copy.121), calls=%async_computation.3 | async-start | bytes 3145728 | tf_op jit(solution)/shard_map/all_to_all | solution.py:181
  187.3 65.0 %all-reduce.6.cloned.1.call-start = ((), (), s32[]{:S(2)}) async-start(), calls=%async_computation.4 | async-start | bytes 3473408 | tf_op jit(solution)/shard_map/psum | solution.py:185
  187.6 8.2 %slice-start = ((s8[6291456]{0:T(1024)(128)(4,1)}), s8[4194304]{0:T(1024)(128)(4,1)S(1)}, s32[]{:S(2)}) async-start(s8[6291456]{0:T(1024)(128)(4,1)} %bitcast.61), calls=%async_computation.5 | async-start | bytes 8388608
  190.4 5.4 %slice-start.1 = ((s8[6291456]{0:T(1024)(128)(4,1)}), s8[2097152]{0:T(1024)(128)(4,1)S(1)}, s32[]{:S(2)}) async-start(s8[6291456]{0:T(1024)(128)(4,1)} %bitcast.61), calls=%async_computation.6 | async-start | bytes 4194304
  190.4 5.4 %copy-start.15 = (bf16[2,3072,256]{2,1,0:T(8,128)(2,1)S(1)}, bf16[2,3072,256]{2,1,0:T(8,128)(2,1)}, u32[]{:S(2)}) copy-start(bf16[2,3072,256]{2,1,0:T(8,128)(2,1)} %copy-done.14) | copy-start | bytes 9437188
  198.1 54.2 %copy-start.5 = (f32[2,848,256]{2,1,0:T(8,128)S(1)}, f32[2,848,256]{2,1,0:T(8,128)}, u32[]{:S(2)}) copy-start(f32[2,848,256]{2,1,0:T(8,128)} %param.20) | copy-start | bytes 5210116
  261.6 17.0 %copy-start.21 = (f32[16,64]{1,0:T(8,128)S(1)}, f32[16,64]{1,0:T(8,128)}, u32[]{:S(2)}) copy-start(f32[16,64]{1,0:T(8,128)} %param.23) | copy-start | bytes 12292
  261.6 17.0 %copy-start.22 = (f32[16,64]{1,0:T(8,128)S(1)}, f32[16,64]{1,0:T(8,128)}, u32[]{:S(2)}) copy-start(f32[16,64]{1,0:T(8,128)} %param.24) | copy-start | bytes 12292
  261.7 16.9 %copy-start.23 = (f32[16,64]{1,0:T(8,128)S(1)}, f32[16,64]{1,0:T(8,128)}, u32[]{:S(2)}) copy-start(f32[16,64]{1,0:T(8,128)} %param.25) | copy-start | bytes 12292
  (10 other events, 19.2 us)
Sparse Core Ops, SparseCore 0:
  205.4 46.8 all-reduce.5
where the time goes:
time: 291 us; the launch traced here: 287 us
  local copies, waits for them, and re-layouts  91.2 us (31%)
  waiting for transfers between devices  89.3 us (31%)
  matrix products  40.9 us (14%)
  other arithmetic  25.4 us (9%)
  starting transfers between devices  15.6 us (5%)
  between operations  14.8 us (5%)
  blocking collectives  9.34 us (3%)
    psum x1, waiting for transfers between devices, shards(): param_grad = lax.psum(local_grad, 'dp')  46.4 us
    all_to_all x1, waiting for transfers between devices, shards(): lax.all_to_all(outgoing, 'expert', split_axis=0, concat_axis=1, tiled=True)  35.9 us
    gather x3, local copies, waits for them, and re-layouts, pick_rows(): return jnp.take(buffer, slot_index, axis=0, mode='fill', fill_value=0)  30.4 us
    unnamed x66, local copies, waits for them, and re-layouts  18.5 us
    scatter x1, other arithmetic, place_rows(): return blank.at[slot_index].set(rows, mode='drop')  13.5 us
    dot_general x4, matrix products, hidden_pass(): jnp.einsum('enr,erw->enw', current, matrix, preferred_element_type=jnp.fl...  13.4 us
    dot_general x4, matrix products, hidden_grads(): jnp.einsum('enr,enw->erw', activations[layer_index], pre_grad, preferred_...  12.7 us
    scatter x1, local copies, waits for them, and re-layouts, place_rows(): return blank.at[slot_index].set(rows, mode='drop')  11.4 us
  transfers between devices with their start and end apart: 4, of which 3 were waited for; matrix products, arithmetic and copies ran while one was open for 8% of the time, Pallas kernels for 0%

commit v1 on v0

--- a/solution.py
+++ b/solution.py
@@ -14,6 +14,14 @@
 ADAM_EPS = 1e-08
 CORRECT_ONE = 1.0 - 0.9**10
 CORRECT_TWO = 1.0 - 0.999**10
+
+
+def sum_by_hops(value, mesh_axis):
+    count, total = (lax.axis_size(mesh_axis), value)
+    for far in [1 << k for k in range(count.bit_length() - 1)]:
+        pairs = [(i, i ^ far) for i in range(count)]
+        total = total + lax.ppermute(total, mesh_axis, pairs)
+    return total
 
 
 def adam_update(param_now, gradient, moment_one, moment_two):
@@ -182,7 +190,7 @@
         code_back, "expert", split_axis=1, concat_axis=0, tiled=True
     ).reshape(slots_all, CODE_WIDTH)
     local_grad = assemble(weight_grads, bias_grads, hidden_grad, code_grad_head, bias_grad_head)
-    param_grad = lax.psum(local_grad, "dp")
+    param_grad = sum_by_hops(local_grad, "dp")
     sample_code_grad = pick_rows(code_slot_grad, slot_index).reshape(ray_rows, SAMPLES, CODE_WIDTH)
     ray_code_grad = jnp.sum(sample_code_grad, axis=1)
     table_grad = lax.dot_general(

time: 291 us -> 259 us (0.89)
  waiting for transfers between devices: 89.3 us -> 75.2 us
  between operations: 14.8 us -> 1.51 us
  matrix products: 40.9 us -> 32.4 us
  other arithmetic: 25.4 us -> 29.5 us
    psum x1 -> x0, waiting for transfers between devices: 46.4 us -> none  [shards(): param_grad = lax.psum(local_grad, 'dp')]
    all_to_all x1, waiting for transfers between devices: 0.01 us -> 32.3 us  [shards(): lax.all_to_all(code_back, 'expert', split_axis=1, concat_axis=0, tiled=True)]
    dot_general x4, matrix products: 12.7 us -> 5.18 us  [hidden_grads(): jnp.einsum('enr,enw->erw', activations[layer_index], pre_grad, preferred_...]
    add x0 -> x1, other arithmetic: none -> 3.41 us  [sum_by_hops(): total = total + lax.ppermute(total, mesh_axis, pairs)]
    unnamed x66 -> x60, local copies, waits for them, and re-layouts: 18.5 us -> 19.2 us
  transfers between devices with their start and end apart: 4 -> 5, of which waited for: 3 -> 3; matrix products, arithmetic and copies ran while one was open for 8% -> 14% of each run, Pallas kernels for 0% -> 0%
where the time goes in v1:
time: 259 us; the launch traced here: 254 us
  local copies, waits for them, and re-layouts  89.5 us (35%)
  waiting for transfers between devices  75.2 us (29%)
  matrix products  32.4 us (13%)
  other arithmetic  29.5 us (11%)
  starting transfers between devices  16.9 us (7%)
  blocking collectives  9.34 us (4%)
    all_to_all x1, waiting for transfers between devices, shards(): lax.all_to_all(outgoing, 'expert', split_axis=0, concat_axis=1, tiled=True)  35.9 us
    all_to_all x1, waiting for transfers between devices, shards(): lax.all_to_all(code_back, 'expert', split_axis=1, concat_axis=0, tiled=True)  32.3 us
    gather x3, local copies, waits for them, and re-layouts, pick_rows(): return jnp.take(buffer, slot_index, axis=0, mode='fill', fill_value=0)  30.6 us
    unnamed x60, local copies, waits for them, and re-layouts  19.2 us
    scatter x1, other arithmetic, place_rows(): return blank.at[slot_index].set(rows, mode='drop')  13.5 us
    dot_general x4, matrix products, hidden_pass(): jnp.einsum('enr,erw->enw', current, matrix, preferred_element_type=jnp.fl...  13.4 us
    scatter x1, local copies, waits for them, and re-layouts, place_rows(): return blank.at[slot_index].set(rows, mode='drop')  11.4 us
    all_to_all x1, blocking collectives, shards(): lax.all_to_all(cot_slots, 'expert', split_axis=0, concat_axis=1, tiled=True)  9.34 us
  transfers between devices with their start and end apart: 5, of which 3 were waited for; matrix products, arithmetic and copies ran while one was open for 14% of the time, Pallas kernels for 0%

profile of v1, /device:TPU:0, one launch (start us, length us, event | category | flops | bytes accessed | tf_op | source)
XLA Modules:
  0.0 254.4 jit_solution(17858865431749198511)
XLA Ops:
  6.9 13.5 %scatter_custom_fusion = bf16[6144,128]{1,0:T(8,128)(2,1)} fusion(s32[4096]{0:T(1024)S(1)} %bitcast.82, bf16[4096,64]{1,0:T(8,128)(2,1)} %bitcast.74, bf16[]{:T(256)} %constant.118, bf16[4096,64]{1,0:T(8,128)(2,1)S(1)} %bitcast.73, bf16[]{:T(256)} %constant.35.clone.1), kind=kCustom, calls=%fused_computation.37 | custom fusion | flops 2097152 | bytes 3145732 | tf_op jit(solution)/shard_map/scatter | solution.py:46
  20.4 7.6 %all-to-all-start = ((bf16[16,384,128]{2,1,0:T(8,128)(2,1)}), bf16[16,384,128]{2,1,0:T(8,128)(2,1)S(1)}, u32[]{:S(2)}, u32[]{:S(2)}) async-start(bf16[16,384,128]{2,1,0:T(8,128)(2,1)} %bitcast.70), calls=%async_computation | async-start | bytes 3145728 | tf_op jit(solution)/shard_map/all_to_all | solution.py:153
  29.1 35.9 %all-to-all-done = bf16[16,384,128]{2,1,0:T(8,128)(2,1)S(1)} async-done(((bf16[16,384,128]{2,1,0:T(8,128)(2,1)}), bf16[16,384,128]{2,1,0:T(8,128)(2,1)S(1)}, u32[]{:S(2)}, u32[]{:S(2)}) %all-to-all-start) | async-done | bytes 1572896 | tf_op jit(solution)/shard_map/all_to_all | solution.py:153
  66.9 4.1 %fusion.2 = (u8[3072,256]{1,0:T(8,128)(4,1)}, f32[2,3072,256]{2,1,0:T(8,128)S(1)}) fusion(f32[2,256]{1,0:T(2,128)S(1)} %bitcast.88, bf16[2,848,256]{2,1,0:T(8,128)(2,1)} %copy-done.8, bf16[2,3072,128]{1,2,0:T(8,128)(2,1)S(1)} %all_to_all.51), kind=kOutput, calls=%fused_computation.32 | convolution fusion | flops 209977344 | bytes 7931904 | tf_op jit(solution)/shard_map/enr,erw->enw/dot_general | solution.py:64
  71.0 3.1 %fusion.3 = (u8[3072,256]{1,0:T(8,128)(4,1)}, f32[2,3072,256]{2,1,0:T(8,128)S(1)}) fusion(f32[2,256]{1,0:T(2,128)S(1)} %get-tuple-element.38, bf16[2,848,256]{2,1,0:T(8,128)(2,1)S(1)} %copy-done.9, f32[2,3072,256]{2,1,0:T(8,128)S(1)} %get-tuple-element.28, f32[2,256]{1,0:T(2,128)S(1)} %bitcast.89), kind=kOutput, calls=%fused_computation.33 | convolution fusion | flops 818675712 | bytes 13635584 | tf_op jit(solution)/shard_map/enr,erw->enw/dot_general | solution.py:64
  74.1 3.1 %fusion.4 = (u8[3072,256]{1,0:T(8,128)(4,1)}, f32[2,3072,256]{2,1,0:T(8,128)S(1)}) fusion(f32[2,256]{1,0:T(2,128)S(1)} %get-tuple-element.37, bf16[2,848,256]{2,1,0:T(8,128)(2,1)S(1)} %copy-done.9, f32[2,3072,256]{2,1,0:T(8,128)S(1)} %get-tuple-element.26, f32[2,256]{1,0:T(2,128)S(1)} %get-tuple-element.38), kind=kOutput, calls=%fused_computation.34 | convolution fusion | flops 818675712 | bytes 13635584 | tf_op jit(solution)/shard_map/enr,erw->enw/dot_general | solution.py:64
  77.2 3.1 %fusion.5 = (u8[3072,256]{1,0:T(8,128)(4,1)}, f32[2,3072,256]{2,1,0:T(8,128)S(1)}) fusion(f32[2,256]{1,0:T(2,128)S(1)} %bitcast.85, bf16[2,848,256]{2,1,0:T(8,128)(2,1)S(1)} %copy-done.9, f32[2,3072,256]{2,1,0:T(8,128)S(1)} %get-tuple-element.24, f32[2,256]{1,0:T(2,128)S(1)} %get-tuple-element.37), kind=kOutput, calls=%fused_computation.35 | convolution fusion | flops 818675712 | bytes 13635584 | tf_op jit(solution)/shard_map/enr,erw->enw/dot_general | solution.py:64
  83.2 2.9 %copy.96 = f32[2,3072,4]{2,0,1:T(2,128)S(1)} copy(f32[2,3072,4]{1,2,0:T(4,128)S(1)} %fusion) | data formatting | bytes 196608 | tf_op jit(solution)/shard_map/add | solution.py:165
  86.1 5.6 %reshape.184 = f32[8,1,3072]{2,1,0:T(1,128)} reshape(f32[3072,2,4]{2,1,0:T(2,128)S(1)} %bitcast.67) | data formatting | bytes 196608
  91.7 4.2 %all-to-all-start.1 = ((f32[8,1,3072]{2,1,0:T(1,128)}), f32[8,1,3072]{2,1,0:T(1,128)S(1)}, u32[]{:S(2)}, u32[]{:S(2)}) async-start(f32[8,1,3072]{2,1,0:T(1,128)} %reshape.184), calls=%async_computation.1 | async-start | bytes 196608 | tf_op jit(solution)/shard_map/all_to_all | solution.py:166
  95.9 7.1 %all-to-all-done.1 = f32[8,1,3072]{2,1,0:T(1,128)S(1)} async-done(((f32[8,1,3072]{2,1,0:T(1,128)}), f32[8,1,3072]{2,1,0:T(1,128)S(1)}, u32[]{:S(2)}, u32[]{:S(2)}) %all-to-all-start.1) | async-done | bytes 98336 | tf_op jit(solution)/shard_map/all_to_all | solution.py:166
  104.4 6.6 %reshape.185 = f32[3072,2,4]{2,1,0:T(2,128)} reshape(f32[8,3072]{1,0:T(8,128)S(1)} %reduce.14) | data formatting | bytes 196608
  113.2 14.2 %gather_fusion = f32[4096,4]{1,0:T(8,128)} fusion(f32[6144,4]{1,0:T(8,128)S(1)} %bitcast.60, s32[4096]{0:T(1024)S(1)} %broadcast_clamp_fusion), kind=kCustom, calls=%fused_computation | custom fusion | bytes 147456 | tf_op jit(solution)/shard_map/jit(_take)/gather | solution.py:50
  131.9 11.4 %scatter_custom_fusion.1 = bf16[6144,4]{1,0:T(8,128)(2,1)S(1)} fusion(s32[4096]{0:T(1024)S(1)} %bitcast.84, bf16[4096,4]{1,0:T(8,128)(2,1)S(1)} %copy.113, bf16[]{:T(256)} %constant.35.clone.1), kind=kCustom, calls=%fused_computation.49 | custom fusion | bytes 49154 | tf_op jit(solution)/shard_map/scatter | solution.py:46
  144.0 9.3 %all_to_all.66 = bf16[16,384,4]{1,2,0:T(4,128)(2,1)S(1)} all-to-all(bf16[16,384,4]{1,2,0:T(4,128)(2,1)S(1)} %copy.114), channel_id=1, replica_groups=mesh['expert'=8,'dp'=4] {'expert'}, dimensions={0} | all-to-all | bytes 98304 | tf_op jit(solution)/shard_map/all_to_all | solution.py:177
  153.4 3.6 %fusion.16 = f32[2,4,256]{2,1,0:T(4,128)S(1)} fusion(bf16[2,3072,4]{1,2,0:T(4,128)(2,1)S(1)} %bitcast.75, f32[2,3072,256]{2,1,0:T(8,128)} %copy-done.3, f32[2,256]{1,0:T(2,128)S(1)} %bitcast.87), kind=kOutput, calls=%fused_computation.47 | convolution fusion | flops 17301504 | bytes 6350848 | tf_op jit(solution)/shard_map/enc,enw->ecw/dot_general | solution.py:180
  170.3 4.5 %concatenate.7 = f32[2,848,256]{2,1,0:T(8,128)} concatenate(f32[2,64,256]{2,1,0:T(8,128)S(1)} %fusion.24, f32[2,256,256]{2,1,0:T(8,128)S(1)} %fusion.10, f32[2,256,256]{2,1,0:T(8,128)S(1)} %fusion.12, f32[2,256,256]{2,1,0:T(8,128)S(1)} %fusion.14, f32[2,4,256]{2,1,0:T(4,128)S(1)} %fusion.16, f32[2,4,256]{2,1,0:T(4,128)S(1)} %pad.16, f32[2,1,256]{2,1,0:T(1,128)S(1)} %broadcast_in_dim.84, ...), dimensions={1} | concatenate | bytes 3473408 | tf_op jit(solution)/shard_map/concatenate | solution.py:104
  177.6 7.1 %copy.121 = f32[2,1536,128]{2,0,1:T(2,128)} copy(f32[2,1536,128]{2,1,0:T(8,128)} %reshape.134) | data formatting | bytes 3145728 | tf_op jit(solution)/shard_map/reshape | solution.py:188
  184.7 3.6 %all-to-all-start.3 = ((f32[2,1536,128]{2,0,1:T(2,128)}), f32[2,1536,128]{2,0,1:T(2,128)S(1)}, u32[]{:S(2)}, u32[]{:S(2)}) async-start(f32[2,1536,128]{2,0,1:T(2,128)} %copy.121), calls=%async_computation.3 | async-start | bytes 3145728 | tf_op jit(solution)/shard_map/all_to_all | solution.py:189
  188.3 3.4 %add.186 = f32[2,848,256]{2,1,0:T(8,128)} add(f32[2,848,256]{2,1,0:T(8,128)} %concatenate.7, f32[2,848,256]{2,1,0:T(8,128)} %collective-permute-done) | non-fusion elementwise | flops 434176 | bytes 5210112 | tf_op jit(solution)/shard_map/add | solution.py:23
  193.9 32.3 %all-to-all-done.3 = f32[2,1536,128]{2,0,1:T(2,128)S(1)} async-done(((f32[2,1536,128]{2,0,1:T(2,128)}), f32[2,1536,128]{2,0,1:T(2,128)S(1)}, u32[]{:S(2)}, u32[]{:S(2)}) %all-to-all-start.3) | async-done | bytes 1572896 | tf_op jit(solution)/shard_map/all_to_all | solution.py:189
  230.0 14.2 %gather_fusion.1 = f32[4096,64]{1,0:T(8,128)} fusion(f32[6144,64]{1,0:T(8,128)S(1)} %reshape.135, s32[4096]{0:T(1024)S(1)} %broadcast_clamp_fusion), kind=kCustom, calls=%fused_computation.1 | custom fusion | bytes 2113536 | tf_op jit(solution)/shard_map/jit(_take)/gather | solution.py:50
  244.2 3.0 %select_reduce_fusion = f32[128,64]{1,0:T(8,128)S(1)} fusion(pred[128,32]{1,0:T(8,128)(4,1)S(1)} %copy.119, f32[4096,64]{1,0:T(8,128)} %gather_fusion.1), kind=kLoop, calls=%fused_computation.28 | loop fusion | flops 516096 | bytes 1085440 | tf_op jit(solution)/shard_map/reduce_sum | solution.py:195
  248.1 6.1 %divide_subtract_fusion = (f32[2,848,256]{2,1,0:T(8,128)}, f32[2,848,256]{2,1,0:T(8,128)}, f32[2,848,256]{2,1,0:T(8,128)}) fusion(f32[2,848,256]{2,1,0:T(8,128)S(1)} %copy-done.5, f32[2,848,256]{2,1,0:T(8,128)} %add.186, f32[2,848,256]{2,1,0:T(8,128)} %collective-permute-done.1, f32[2,848,256]{2,1,0:T(8,128)} %param.21, f32[2,848,256]{2,1,0:T(8,128)} %param.22), kind=kLoop, calls=%fused_computation.30 | loop fusion | flops 5644288 | bytes 13893632 | tf_op jit(solution)/shard_map/sub | solution.py:31
  (140 shorter events, 43.6 us)
Async XLA Ops:
  6.9 21.2 %copy-start.4 = (f32[2,848,256]{2,1,0:T(8,128)S(1)}, f32[2,848,256]{2,1,0:T(8,128)}, u32[]{:S(2)}) copy-start(f32[2,848,256]{2,1,0:T(8,128)} %param.20) | copy-start | bytes 5210116
  20.4 44.6 %all-to-all-start = ((bf16[16,384,128]{2,1,0:T(8,128)(2,1)}), bf16[16,384,128]{2,1,0:T(8,128)(2,1)S(1)}, u32[]{:S(2)}, u32[]{:S(2)}) async-start(bf16[16,384,128]{2,1,0:T(8,128)(2,1)} %bitcast.70), calls=%async_computation | async-start | bytes 3145728 | tf_op jit(solution)/shard_map/all_to_all | solution.py:153
  66.9 16.1 %copy-start.6 = (bf16[2,3072,128]{1,2,0:T(8,128)(2,1)}, bf16[2,3072,128]{1,2,0:T(8,128)(2,1)S(1)}, u32[]{:S(2)}) copy-start(bf16[2,3072,128]{1,2,0:T(8,128)(2,1)S(1)} %all_to_all.51) | copy-start | bytes 4718596
  66.9 4.1 %copy-start.9 = (bf16[2,848,256]{2,1,0:T(8,128)(2,1)S(1)}, bf16[2,848,256]{2,1,0:T(8,128)(2,1)}, u32[]{:S(2)}) copy-start(bf16[2,848,256]{2,1,0:T(8,128)(2,1)} %copy-done.8) | copy-start | bytes 2605060
  71.0 3.1 %copy-start = (f32[2,3072,256]{2,1,0:T(8,128)}, f32[2,3072,256]{2,1,0:T(8,128)S(1)}, u32[]{:S(2)}) copy-start(f32[2,3072,256]{2,1,0:T(8,128)S(1)} %get-tuple-element.28) | copy-start | bytes 18874372
  74.1 3.1 %copy-start.1 = (f32[2,3072,256]{2,1,0:T(8,128)}, f32[2,3072,256]{2,1,0:T(8,128)S(1)}, u32[]{:S(2)}) copy-start(f32[2,3072,256]{2,1,0:T(8,128)S(1)} %get-tuple-element.26) | copy-start | bytes 18874372
  77.2 3.1 %copy-start.2 = (f32[2,3072,256]{2,1,0:T(8,128)}, f32[2,3072,256]{2,1,0:T(8,128)S(1)}, u32[]{:S(2)}) copy-start(f32[2,3072,256]{2,1,0:T(8,128)S(1)} %get-tuple-element.24) | copy-start | bytes 18874372
  80.4 2.6 %copy-start.3 = (f32[2,3072,256]{2,1,0:T(8,128)}, f32[2,3072,256]{2,1,0:T(8,128)S(1)}, u32[]{:S(2)}) copy-start(f32[2,3072,256]{2,1,0:T(8,128)S(1)} %get-tuple-element.22) | copy-start | bytes 18874372
  91.7 11.3 %all-to-all-start.1 = ((f32[8,1,3072]{2,1,0:T(1,128)}), f32[8,1,3072]{2,1,0:T(1,128)S(1)}, u32[]{:S(2)}, u32[]{:S(2)}) async-start(f32[8,1,3072]{2,1,0:T(1,128)} %reshape.184), calls=%async_computation.1 | async-start | bytes 196608 | tf_op jit(solution)/shard_map/all_to_all | solution.py:166
  113.2 16.7 %copy-start.15 = (f32[128,32]{0,1:T(8,128)S(1)}, f32[128,32]{0,1:T(8,128)}, u32[]{:S(2)}) copy-start(f32[128,32]{0,1:T(8,128)} %param.14) | copy-start | bytes 49156
  113.2 16.7 %copy-start.19 = (s32[128]{0:T(128)S(1)}, s32[128]{0:T(128)}, u32[]{:S(2)}) copy-start(s32[128]{0:T(128)} %param.16) | copy-start | bytes 1540
  127.5 2.9 %copy-start.20 = (f32[3,128]{1,0:T(4,128)S(1)}, f32[3,128]{1,0:T(4,128)}, u32[]{:S(2)}) copy-start(f32[3,128]{1,0:T(4,128)} %param.15) | copy-start | bytes 4612
  153.4 3.6 %copy-start.7 = (bf16[2,3072,128]{1,2,0:T(8,128)(2,1)S(1)}, bf16[2,3072,128]{1,2,0:T(8,128)(2,1)}, u32[]{:S(2)}) copy-start(bf16[2,3072,128]{1,2,0:T(8,128)(2,1)} %copy-done.6) | copy-start | bytes 4718596
  153.4 4.0 %copy-start.10 = (bf16[2,848,256]{2,1,0:T(8,128)(2,1)S(1)}, bf16[2,848,256]{2,1,0:T(8,128)(2,1)}, u32[]{:S(2)}) copy-start(bf16[2,848,256]{2,1,0:T(8,128)(2,1)} %copy-done.8) | copy-start | bytes 2605060
  153.4 4.0 %copy-start.14 = (u8[3072,256]{1,0:T(8,128)(4,1)S(1)}, u8[3072,256]{1,0:T(8,128)(4,1)}, u32[]{:S(2)}) copy-start(u8[3072,256]{1,0:T(8,128)(4,1)} %get-tuple-element.21) | copy-start | bytes 2359300
  160.0 2.9 %slice-start.2 = ((s8[6291456]{0:T(1024)(128)(4,1)}), s8[4194304]{0:T(1024)(128)(4,1)S(1)}, s32[]{:S(2)}) async-start(s8[6291456]{0:T(1024)(128)(4,1)} %bitcast.63), calls=%async_computation.6 | async-start | bytes 8388608
  163.3 2.9 %slice-start = ((s8[6291456]{0:T(1024)(128)(4,1)}), s8[4194304]{0:T(1024)(128)(4,1)S(1)}, s32[]{:S(2)}) async-start(s8[6291456]{0:T(1024)(128)(4,1)} %bitcast.61), calls=%async_computation.4 | async-start | bytes 8388608
  174.7 13.6 %collective-permute-start = (f32[2,848,256]{2,1,0:T(8,128)}, f32[2,848,256]{2,1,0:T(8,128)}, u32[]{:S(2)}, u32[]{:S(2)}) collective-permute-start(f32[2,848,256]{2,1,0:T(8,128)} %concatenate.7), channel_id=1, source_target_pairs={{0,1},{1,0},{2,3},{3,2},{4,5},{5,4},{6,7},{7,6},{8,9},{9,8},{10,11... | collective-permute-start | bytes 5210120 | tf_op jit(solution)/shard_map/ppermute | solution.py:23
  184.7 41.5 %all-to-all-start.3 = ((f32[2,1536,128]{2,0,1:T(2,128)}), f32[2,1536,128]{2,0,1:T(2,128)S(1)}, u32[]{:S(2)}, u32[]{:S(2)}) async-start(f32[2,1536,128]{2,0,1:T(2,128)} %copy.121), calls=%async_computation.3 | async-start | bytes 3145728 | tf_op jit(solution)/shard_map/all_to_all | solution.py:189
  191.7 56.3 %collective-permute-start.1 = (f32[2,848,256]{2,1,0:T(8,128)}, f32[2,848,256]{2,1,0:T(8,128)}, u32[]{:S(2)}, u32[]{:S(2)}) collective-permute-start(f32[2,848,256]{2,1,0:T(8,128)} %add.186), channel_id=1, source_target_pairs={{0,2},{1,3},{2,0},{3,1},{4,6},{5,7},{6,4},{7,5},{8,10},{9,11},{10,... | collective-permute-start | bytes 5210120 | tf_op jit(solution)/shard_map/ppermute | solution.py:23
  230.0 17.2 %copy-start.16 = (f32[16,64]{1,0:T(8,128)S(1)}, f32[16,64]{1,0:T(8,128)}, u32[]{:S(2)}) copy-start(f32[16,64]{1,0:T(8,128)} %param.23) | copy-start | bytes 12292
  230.0 17.2 %copy-start.17 = (f32[16,64]{1,0:T(8,128)S(1)}, f32[16,64]{1,0:T(8,128)}, u32[]{:S(2)}) copy-start(f32[16,64]{1,0:T(8,128)} %param.24) | copy-start | bytes 12292
  230.0 17.2 %copy-start.18 = (f32[16,64]{1,0:T(8,128)S(1)}, f32[16,64]{1,0:T(8,128)}, u32[]{:S(2)}) copy-start(f32[16,64]{1,0:T(8,128)} %param.25) | copy-start | bytes 12292
  244.1 3.9 %copy-start.5 = (f32[2,848,256]{2,1,0:T(8,128)S(1)}, f32[2,848,256]{2,1,0:T(8,128)}, u32[]{:S(2)}) copy-start(f32[2,848,256]{2,1,0:T(8,128)} %param.20) | copy-start | bytes 5210116
  (8 other events, 13.9 us)
